TPU v7x, 32 devices: a whole 2x2x4 slice. The times are simulated.
32 devices in a mesh: ba: 4 (over z), aa: 8 (over y, x, core).
Axes of the slice: x: 2, y: 2, z: 4, core: 2. Of those that a mesh axis runs over, the one named last changes fastest.
Arguments:
- tokens: bfloat16 [6144, 1024], P(('ba', 'aa')), parts along dimension 0, may hold values from -6 to 6
- latents: bfloat16 [1024, 1024], P(('ba', 'aa')), parts along dimension 0, may hold values from -6 to 6
- read_query: bfloat16 [1024, 512], replicated, may hold values from -0.1875 to 0.1875
- read_keyval: bfloat16 [1024, 1024], replicated, may hold values from -0.1875 to 0.1875
- read_out: bfloat16 [512, 1024], replicated, may hold values from -0.25 to 0.25
- self_qkv: bfloat16 [1024, 1536], replicated, may hold values from -0.1875 to 0.1875
- self_out: bfloat16 [512, 1024], replicated, may hold values from -0.25 to 0.25
- write_query: bfloat16 [1024, 512], replicated, may hold values from -0.1875 to 0.1875
- write_keyval: bfloat16 [1024, 1024], replicated, may hold values from -0.1875 to 0.1875
- write_out: bfloat16 [512, 1024], replicated, may hold values from -0.25 to 0.25
- qk_gain: float32 [6, 512], replicated, may hold values from 0.8 to 2.2
Outputs:
- tokens_out: bfloat16 [6144, 1024], P(('ba', 'aa')), parts along dimension 0
- latents_out: bfloat16 [1024, 1024], P(('ba', 'aa')), parts along dimension 0
There are 4 independent parts, one for each index of `ba`. A program takes and returns all parts, laid end to end along the dimension named above; an argument that names none is the same for every part. Nothing has to cross between parts.
All inputs are finite; a program needn't handle non-finite values.
Results may differ from a plain program's by a relative error of at most 0.014.
Values may be sent and summed in bfloat16 or wider, within the bound.
A program may use at most 64 MiB of HBM per device.

v0:
```python
import math

import jax
import jax.numpy as jnp
from jax import lax
from jax.sharding import PartitionSpec as P

HEADS = 8


EPSILON = 1e-06


def rms_rows(values):
    widened = values.astype(jnp.float32)
    return (
        widened * lax.rsqrt(jnp.mean(widened * widened, axis=-1, keepdims=True) + EPSILON)
    ).astype(jnp.bfloat16)


def head_norm(projected, gain_row, head_count):
    row_count = projected.shape[0]
    split_heads = projected.reshape(row_count, head_count, -1)
    normed = split_heads * lax.rsqrt(
        jnp.mean(split_heads * split_heads, axis=-1, keepdims=True) + EPSILON
    )
    return (normed.reshape(row_count, -1) * gain_row).astype(jnp.bfloat16)


def attend_block(query_rows, key_rows, value_rows, head_count):
    row_count = query_rows.shape[0]
    query_heads = query_rows.reshape(row_count, head_count, -1)
    key_heads = key_rows.reshape(key_rows.shape[0], head_count, -1)
    value_heads = value_rows.reshape(value_rows.shape[0], head_count, -1)
    score_scale = 1.0 / math.sqrt(query_heads.shape[2])
    scores = (
        jnp.einsum("qhe,khe->hqk", query_heads, key_heads, preferred_element_type=jnp.float32)
        * score_scale
    )
    weights = jnp.exp(scores)
    denominator = jnp.sum(weights, axis=2).T
    numerator = jnp.einsum(
        "hqk,khe->qhe",
        weights.astype(jnp.bfloat16),
        value_heads,
        preferred_element_type=jnp.float32,
    )
    return (numerator.reshape(row_count, -1), denominator)


def partial_attend(query_rows, key_rows, value_rows, head_count):
    row_count = query_rows.shape[0]
    if row_count > 512 and row_count % 512 == 0:
        blocks = query_rows.reshape(row_count // 512, 512, query_rows.shape[1])
        numerator, denominator = lax.map(
            lambda one_block: attend_block(one_block, key_rows, value_rows, head_count), blocks
        )
        return (numerator.reshape(row_count, -1), denominator.reshape(row_count, head_count))
    return attend_block(query_rows, key_rows, value_rows, head_count)


def finish_heads(numerator, denominator, head_count):
    row_count = numerator.shape[0]
    quotient = numerator.reshape(row_count, head_count, -1) / denominator[:, :, None]
    return quotient.reshape(row_count, -1).astype(jnp.bfloat16)


def attention(query_rows, key_rows, value_rows, head_count):
    numerator, denominator = partial_attend(query_rows, key_rows, value_rows, head_count)
    return finish_heads(numerator, denominator, head_count)


def residual_add(base, attended, projection):
    update = jnp.dot(attended, projection, preferred_element_type=jnp.float32)
    return (base.astype(jnp.float32) + update).astype(jnp.bfloat16)


def self_block(read_latents, self_qkv, qk_gain, inner_width):
    triple = jnp.dot(rms_rows(read_latents), self_qkv, preferred_element_type=jnp.float32)
    self_queries = head_norm(triple[:, :inner_width], qk_gain[2], HEADS)
    self_keys = head_norm(triple[:, inner_width : 2 * inner_width], qk_gain[3], HEADS)
    self_values = triple[:, 2 * inner_width :].astype(jnp.bfloat16)
    return (self_queries, self_keys, self_values)


def write_pairs(latent_rows, write_keyval, qk_gain, inner_width):
    latent_pairs = jnp.dot(rms_rows(latent_rows), write_keyval, preferred_element_type=jnp.float32)
    write_keys = head_norm(latent_pairs[:, :inner_width], qk_gain[5], HEADS)
    write_values = latent_pairs[:, inner_width:].astype(jnp.bfloat16)
    return (write_keys, write_values)


def per_device(
    tokens,
    latents,
    read_query,
    read_keyval,
    read_out,
    self_qkv,
    self_out,
    write_query,
    write_keyval,
    write_out,
    qk_gain,
):
    inner_width = read_query.shape[1]
    own_count = latents.shape[0]
    first_row = lax.axis_index("aa") * own_count
    normed_tokens = rms_rows(tokens)
    token_pairs = jnp.dot(normed_tokens, read_keyval, preferred_element_type=jnp.float32)
    read_keys = head_norm(token_pairs[:, :inner_width], qk_gain[1], HEADS)
    read_values = token_pairs[:, inner_width:].astype(jnp.bfloat16)
    every_latent = lax.all_gather(latents, "aa", axis=0, tiled=True)
    read_queries = head_norm(
        jnp.dot(rms_rows(every_latent), read_query, preferred_element_type=jnp.float32),
        qk_gain[0],
        HEADS,
    )
    numerator, denominator = partial_attend(read_queries, read_keys, read_values, HEADS)
    numerator, denominator = lax.psum((numerator, denominator), "aa")
    all_read = residual_add(every_latent, finish_heads(numerator, denominator, HEADS), read_out)
    write_queries = head_norm(
        jnp.dot(normed_tokens, write_query, preferred_element_type=jnp.float32), qk_gain[4], HEADS
    )
    self_queries, self_keys, self_values = self_block(all_read, self_qkv, qk_gain, inner_width)
    self_attended = attention(self_queries, self_keys, self_values, HEADS)
    all_updated = residual_add(all_read, self_attended, self_out)
    write_keys, write_values = write_pairs(all_updated, write_keyval, qk_gain, inner_width)
    latents_out = lax.dynamic_slice_in_dim(all_updated, first_row, own_count, 0)
    write_attended = attention(write_queries, write_keys, write_values, HEADS)
    tokens_out = residual_add(tokens, write_attended, write_out)
    return (tokens_out, latents_out)


def solution(mesh):
    placed = (
        P(("ba", "aa"), None),
        P(("ba", "aa"), None),
        P(),
        P(),
        P(),
        P(),
        P(),
        P(),
        P(),
        P(),
        P(),
    )
    return jax.shard_map(
        per_device,
        mesh=mesh,
        in_specs=placed,
        out_specs=(P(("ba", "aa"), None), P(("ba", "aa"), None)),
        check_vma=False,
    )
```

profile of v0, /device:TPU:0, one launch (start us, length us, event | category | flops | bytes accessed | tf_op | source)
XLA Modules:
  0.0 164.5 jit_solution(1211361876414118551)
XLA Ops:
  8.5 2.3 %fusion.34 = f32[192,1024]{1,0:T(8,128)S(1)} fusion(bf16[1024,1024]{1,0:T(8,128)(2,1)} %param.14, bf16[192,1024]{1,0:T(8,128)(2,1)} %param.11, f32[192]{0:T(256)S(1)} %add_rsqrt_fusion.9), kind=kOutput, calls=%fused_computation.65 | convolution fusion | flops 403243008 | bytes 3277568 | tf_op jit(solution)/shard_map/dot_general | solution.py:110
  11.9 1.8 %copy.23 = bf16[192,512]{0,1:T(8,128)(2,1)} copy(bf16[192,512]{1,0:T(8,128)(2,1)} %slice.75) | data formatting | bytes 393216 | tf_op jit(solution)/shard_map/slice | solution.py:112
  13.7 11.6 %all_gather.3 = bf16[256,1024]{1,0:T(8,128)(2,1)S(1)} all-gather(bf16[32,1024]{1,0:T(8,128)(2,1)} %param.12), channel_id=1, replica_groups=mesh['ba'=4,'aa'=8] {'aa'}, dimensions={0}, use_global_device_ids=true | all-gather | bytes 589824 | tf_op jit(solution)/shard_map/all_gather | solution.py:113
  26.1 2.7 %fusion.38 = (f32[256,512]{1,0:T(8,128)}, f32[256,512]{1,0:T(8,128)}) fusion(bf16[1024,512]{1,0:T(8,128)(2,1)} %param.13, bf16[256,1024]{1,0:T(8,128)(2,1)S(1)} %all_gather.3, f32[256]{0:T(256)S(1)} %add_rsqrt_fusion.8), kind=kOutput, calls=%fused_computation.79 | convolution fusion | flops 269352960 | bytes 2622464 | tf_op jit(solution)/shard_map/dot_general | solution.py:115
  28.8 2.0 %copy.24 = f32[256,512]{0,1:T(8,128)} copy(f32[256,512]{1,0:T(8,128)} %get-tuple-element.12) | data formatting | bytes 1048576 | tf_op jit(solution)/shard_map/mul | solution.py:25
  32.8 2.1 %copy.25 = f32[256,512]{1,0:T(8,128)} copy(f32[256,512]{0,1:T(8,128)} %bitcast.82) | data formatting | bytes 1048576 | tf_op jit(solution)/shard_map/mul | solution.py:24
  36.3 2.0 %multiply_convert_fusion.3 = bf16[256,512]{1,0:T(8,128)(2,1)} fusion(f32[256,512]{1,0:T(8,128)} %get-tuple-element.13, f32[256,512]{1,0:T(8,128)} %copy.25, f32[512]{0:T(512)S(1)} %bitcast.102), kind=kLoop, calls=%fused_computation.55 | loop fusion | flops 393216 | bytes 1312768 | tf_op jit(solution)/shard_map/convert_element_type | solution.py:27
  38.4 1.8 %copy.26 = bf16[256,512]{0,1:T(8,128)(2,1)} copy(bf16[256,512]{1,0:T(8,128)(2,1)} %multiply_convert_fusion.3) | data formatting | bytes 524288 | tf_op jit(solution)/shard_map/convert_element_type | solution.py:27
  46.1 1.8 %copy.29 = bf16[192,512]{0,1:T(8,128)(2,1)} copy(bf16[192,512]{1,0:T(8,128)(2,1)} %multiply_convert_fusion.5) | data formatting | bytes 393216 | tf_op jit(solution)/shard_map/convert_element_type | solution.py:27
  48.0 2.1 %fusion.39 = (f32[8,256]{1,0:T(8,128)}, bf16[8,256,192]{1,2,0:T(8,128)(2,1)S(1)}) fusion(bf16[256,8,64]{0,2,1:T(8,128)(2,1)} %bitcast.93, bf16[192,8,64]{0,2,1:T(8,128)(2,1)} %bitcast.90), kind=kOutput, calls=%fused_computation.80 | convolution fusion | flops 51509248 | bytes 1253376 | tf_op jit(solution)/shard_map/qhe,khe->hqk/dot_general | solution.py:37
  50.1 2.0 %fusion.20 = f32[8,64,256]{2,1,0:T(8,128)} fusion(bf16[192,8,64]{0,2,1:T(8,128)(2,1)} %bitcast.88, bf16[8,256,192]{1,2,0:T(8,128)(2,1)S(1)} %get-tuple-element.15), kind=kOutput, calls=%fused_computation.35 | convolution fusion | flops 50331648 | bytes 1507328 | tf_op jit(solution)/shard_map/hqk,khe->qhe/dot_general | solution.py:42
  52.1 2.5 %fusion.40 = (f32[192,512]{1,0:T(8,128)}, f32[192,512]{1,0:T(8,128)}) fusion(bf16[1024,512]{1,0:T(8,128)(2,1)} %param.18, bf16[192,1024]{1,0:T(8,128)(2,1)S(1)} %copy-done.2, f32[192]{0:T(256)S(1)} %add_rsqrt_fusion.9), kind=kOutput, calls=%fused_computation.81 | convolution fusion | flops 202014720 | bytes 2228992 | tf_op jit(solution)/shard_map/dot_general | solution.py:123
  54.7 2.0 %copy.39 = f32[192,512]{0,1:T(8,128)} copy(f32[192,512]{1,0:T(8,128)} %get-tuple-element.22) | data formatting | bytes 786432 | tf_op jit(solution)/shard_map/mul | solution.py:25
  58.6 2.0 %copy.40 = f32[192,512]{1,0:T(8,128)} copy(f32[192,512]{0,1:T(8,128)} %bitcast.81) | data formatting | bytes 786432 | tf_op jit(solution)/shard_map/mul | solution.py:24
  60.6 1.9 %multiply_convert_fusion.4 = bf16[192,512]{1,0:T(8,128)(2,1)} fusion(f32[192,512]{1,0:T(8,128)} %get-tuple-element.23, f32[192,512]{1,0:T(8,128)} %copy.40, f32[512]{0:T(512)S(1)} %bitcast.100), kind=kLoop, calls=%fused_computation.61 | loop fusion | flops 294912 | bytes 985088 | tf_op jit(solution)/shard_map/convert_element_type | solution.py:27
  62.5 1.8 %copy.41 = bf16[192,512]{0,1:T(8,128)(2,1)} copy(bf16[192,512]{1,0:T(8,128)(2,1)} %multiply_convert_fusion.4) | data formatting | bytes 393216 | tf_op jit(solution)/shard_map/convert_element_type | solution.py:27
  64.2 13.6 %psum.15 = f32[256,8]{0,1:T(8,128)S(1)} all-reduce(f32[256,8]{0,1:T(8,128)} %bitcast.103), channel_id=1, replica_groups=mesh['ba'=4,'aa'=8] {'aa'}, use_global_device_ids=true, to_apply=%region_6.0 | all-reduce | flops 2048 | bytes 16384 | tf_op jit(solution)/shard_map/psum | solution.py:120
  77.8 29.6 %all-reduce.2.cloned.1.call-done = f32[256,512]{0,1:T(8,128)} async-done(((f32[256,512]{0,1:T(8,128)}), f32[256,512]{0,1:T(8,128)}) %all-reduce.2.cloned.1.call-update) | async-done | bytes 524304 | tf_op jit(solution)/shard_map/psum | solution.py:120
  108.5 1.9 %fusion.13 = (f32[256]{0:T(256)S(1)}, bf16[256,1024]{1,0:T(8,128)(2,1)S(1)}) fusion(bf16[256,512]{0,1:T(8,128)(2,1)S(1)} %fusion.28, bf16[512,1024]{1,0:T(8,128)(2,1)} %param.15, bf16[256,1024]{1,0:T(8,128)(2,1)} %copy-done.4), kind=kOutput, calls=%fused_computation.29 | convolution fusion | flops 270008064 | bytes 2360320 | tf_op jit(solution)/shard_map/dot_general | solution.py:74
  113.8 1.8 %copy.30 = bf16[256,512]{0,1:T(8,128)(2,1)} copy(bf16[256,512]{1,0:T(8,128)(2,1)} %slice.74) | data formatting | bytes 524288 | tf_op jit(solution)/shard_map/slice | solution.py:82
  115.6 2.0 %copy.34 = f32[256,512]{0,1:T(8,128)} copy(f32[256,512]{1,0:T(8,128)} %get-tuple-element.4) | data formatting | bytes 1048576 | tf_op jit(solution)/shard_map/mul | solution.py:25
  119.5 2.0 %copy.35 = f32[256,512]{1,0:T(8,128)} copy(f32[256,512]{0,1:T(8,128)} %bitcast.83) | data formatting | bytes 1048576 | tf_op jit(solution)/shard_map/mul | solution.py:24
  121.6 2.0 %copy.31 = f32[256,512]{0,1:T(8,128)} copy(f32[256,512]{1,0:T(8,128)} %get-tuple-element.5) | data formatting | bytes 1048576 | tf_op jit(solution)/shard_map/mul | solution.py:25
  125.6 2.1 %copy.32 = f32[256,512]{1,0:T(8,128)} copy(f32[256,512]{0,1:T(8,128)} %bitcast.84) | data formatting | bytes 1048576 | tf_op jit(solution)/shard_map/mul | solution.py:24
  127.6 2.6 %multiply_convert_fusion.1 = (bf16[256,512]{1,0:T(8,128)(2,1)}, bf16[256,512]{1,0:T(8,128)(2,1)}) fusion(f32[256,512]{1,0:T(8,128)} %copy.35, f32[256,1536]{1,0:T(8,128)} %copy-done.1, f32[512]{0:T(512)S(1)} %bitcast.98, f32[512]{0:T(512)S(1)} %bitcast.99, f32[256,512]{1,0:T(8,128)} %copy.32), kind=kLoop, calls=%fused_computation.52 | loop fusion | flops 786432 | bytes 2625536 | tf_op jit(solution)/shard_map/convert_element_type | solution.py:27
  130.2 1.8 %copy.33 = bf16[256,512]{0,1:T(8,128)(2,1)} copy(bf16[256,512]{1,0:T(8,128)(2,1)} %get-tuple-element.3) | data formatting | bytes 524288 | tf_op jit(solution)/shard_map/convert_element_type | solution.py:27
  132.0 1.8 %copy.36 = bf16[256,512]{0,1:T(8,128)(2,1)} copy(bf16[256,512]{1,0:T(8,128)(2,1)} %get-tuple-element.2) | data formatting | bytes 524288 | tf_op jit(solution)/shard_map/convert_element_type | solution.py:27
  140.3 1.8 %copy.38 = bf16[256,512]{0,1:T(8,128)(2,1)} copy(bf16[256,512]{1,0:T(8,128)(2,1)} %slice.73) | data formatting | bytes 524288 | tf_op jit(solution)/shard_map/slice | solution.py:89
  142.1 2.0 %copy.42 = f32[256,512]{0,1:T(8,128)} copy(f32[256,512]{1,0:T(8,128)} %slice_multiply_fusion) | data formatting | bytes 1048576 | tf_op jit(solution)/shard_map/mul | solution.py:25
  146.1 2.1 %copy.43 = f32[256,512]{1,0:T(8,128)} copy(f32[256,512]{0,1:T(8,128)} %bitcast.85) | data formatting | bytes 1048576 | tf_op jit(solution)/shard_map/mul | solution.py:24
  148.1 2.0 %multiply_convert_fusion = bf16[256,512]{1,0:T(8,128)(2,1)} fusion(f32[256,512]{1,0:T(8,128)} %copy.43, f32[256,1024]{1,0:T(8,128)} %copy-done.3, f32[512]{0:T(512)S(1)} %bitcast.97), kind=kLoop, calls=%fused_computation.50 | loop fusion | flops 393216 | bytes 1312768 | tf_op jit(solution)/shard_map/convert_element_type | solution.py:27
  150.1 1.8 %copy.44 = bf16[256,512]{0,1:T(8,128)(2,1)} copy(bf16[256,512]{1,0:T(8,128)(2,1)} %multiply_convert_fusion) | data formatting | bytes 524288 | tf_op jit(solution)/shard_map/convert_element_type | solution.py:27
  (74 shorter events, 36.9 us)
Async XLA Ops:
  7.2 103.3 %copy-start = (bf16[1024,1536]{1,0:T(8,128)(2,1)S(1)}, bf16[1024,1536]{1,0:T(8,128)(2,1)}, u32[]{:S(2)}) copy-start(bf16[1024,1536]{1,0:T(8,128)(2,1)} %param.16) | copy-start | bytes 9437188
  7.2 100.2 %all-reduce.2.cloned.1.call-start = ((), (), s32[]{:S(2)}) async-start(), calls=%async_computation | async-start | bytes 1048576 | tf_op jit(solution)/shard_map/psum | solution.py:120
  10.9 1.0 copy-start.5
  25.3 0.8 copy-start.4
  46.1 6.0 %copy-start.2 = (bf16[192,1024]{1,0:T(8,128)(2,1)S(1)}, bf16[192,1024]{1,0:T(8,128)(2,1)}, u32[]{:S(2)}) copy-start(bf16[192,1024]{1,0:T(8,128)(2,1)} %param.11) | copy-start | bytes 1179652
  110.4 1.1 copy-start.9
  111.5 1.2 copy-start.1
  119.5 8.1 %copy-start.12 = (f32[1,512]{1,0:T(1,128)S(1)}, f32[1,512]{1,0:T(1,128)}, u32[]{:S(2)}) copy-start(f32[1,512]{1,0:T(1,128)} %get-tuple-element.8) | copy-start | bytes 6148
  133.8 1.6 copy-start.11
  135.4 1.0 copy-start.10
  135.4 1.4 copy-start.13
  135.9 1.7 %copy-start.6 = (bf16[1024,1024]{1,0:T(8,128)(2,1)S(1)}, bf16[1024,1024]{1,0:T(8,128)(2,1)}, u32[]{:S(2)}) copy-start(bf16[1024,1024]{1,0:T(8,128)(2,1)} %param.19) | copy-start | bytes 6291460
  137.4 1.8 %copy-start.8 = (bf16[256,1024]{1,0:T(8,128)(2,1)}, bf16[256,1024]{1,0:T(8,128)(2,1)S(1)}, u32[]{:S(2)}) copy-start(bf16[256,1024]{1,0:T(8,128)(2,1)S(1)} %get-tuple-element.21) | copy-start | bytes 1572868
  138.4 1.1 copy-start.3
  153.4 3.1 %copy-start.7 = (bf16[512,1024]{1,0:T(8,128)(2,1)S(1)}, bf16[512,1024]{1,0:T(8,128)(2,1)}, u32[]{:S(2)}) copy-start(bf16[512,1024]{1,0:T(8,128)(2,1)} %param.20) | copy-start | bytes 3145732
Sparse Core Ops, SparseCore 0:
  52.3 55.0 all-reduce.1
where the time goes:
time: 166 us; the launch traced here: 165 us
  local copies, waits for them, and re-layouts  51.8 us (31%)
  waiting for transfers between devices  29.6 us (18%)
  blocking collectives  25.2 us (15%)
  matrix products  22.3 us (13%)
  other arithmetic  21.3 us (13%)
  between operations  14.3 us (9%)
    psum x1, waiting for transfers between devices, per_device(): numerator, denominator = lax.psum((numerator, denominator), 'aa')  29.6 us
    mul x12, local copies, waits for them, and re-layouts, head_norm(): split_heads * lax.rsqrt(jnp.mean(split_heads * split_heads, axis=-1, keep...  16.5 us
    psum x1, blocking collectives, per_device(): numerator, denominator = lax.psum((numerator, denominator), 'aa')  13.6 us
    all_gather x1, blocking collectives, per_device(): every_latent = lax.all_gather(latents, 'aa', axis=0, tiled=True)  11.6 us
    mul x6, local copies, waits for them, and re-layouts, head_norm(): split_heads * split_heads  11.2 us
    convert_element_type x6, local copies, waits for them, and re-layouts, head_norm(): return (normed.reshape(row_count, -1) * gain_row).astype(jnp.bfloat16)  10.8 us
    convert_element_type x5, other arithmetic, head_norm(): return (normed.reshape(row_count, -1) * gain_row).astype(jnp.bfloat16)  10.2 us
    reduce_sum x6, other arithmetic, head_norm(): jnp.mean(split_heads * split_heads, axis=-1, keepdims=True) + EPSILON  6.54 us
  transfers between devices with their start and end apart: 1, of which 1 were waited for; matrix products, arithmetic and copies ran while one was open for 7% of the time, Pallas kernels for 0%

commit v1 on v0

v1 whole, which is shorter than its diff:
```python
import functools
import math

import jax
import jax.numpy as jnp
from jax import lax
from jax.experimental import pallas as pl
from jax.experimental.pallas import tpu as pltpu
from jax.sharding import PartitionSpec as P

HEADS = 8
EPSILON = 1e-06
MESH = pl.DeviceIdType.MESH
TILE = 256
LANES = 128
F32 = jnp.float32
BF16 = jnp.bfloat16


def dot(a, b):
    return jnp.dot(a, b, preferred_element_type=F32)


def dot_nt(a, b):
    return lax.dot_general(a, b, (((1,), (1,)), ((), ())), preferred_element_type=F32)


def rms(x):
    x = x.astype(F32)
    return (x * lax.rsqrt(jnp.mean(x * x, axis=-1, keepdims=True) + EPSILON)).astype(BF16)


def row_blocks(rows, body):
    block = min(rows, TILE)
    if rows == block:
        body(pl.ds(0, block))
    else:

        def step(i, carry):
            body(pl.ds(pl.multiple_of(i * block, block), block))
            return carry

        lax.fori_loop(0, rows // block, step, 0)


def kernel(
    n,
    tokens,
    latents,
    w_rq,
    w_rkv,
    w_ro,
    w_sqkv,
    w_so,
    w_wq,
    w_wkv,
    w_wo,
    gain,
    tok_out,
    lat_out,
    tok,
    lat_all,
    b_rq,
    b_rkv,
    b_ro,
    b_sqkv,
    b_so,
    b_wq,
    b_wkv,
    b_wo,
    ntok,
    rk,
    rv,
    wq,
    rq,
    part,
    recv,
    att,
    rlat,
    normed,
    sq,
    sk,
    sv,
    wk,
    wv,
    mean_mat,
    load_sem,
    send_sem,
    recv_sem,
):
    me = lax.axis_index("aa")
    own = latents.shape[0]
    every = n * own
    inner = w_rq.shape[1]
    width = inner // HEADS
    tiles = inner // TILE
    d = tokens.shape[1]
    pairs = inner // LANES

    mine = pl.ds(pl.multiple_of(me * own, own), own)
    loads = []
    order = (
        (latents, lat_all.at[mine]),
        (tokens, tok),
        (w_rkv, b_rkv),
        (w_rq, b_rq),
        (w_wq, b_wq),
        (w_ro, b_ro),
        (w_sqkv, b_sqkv),
        (w_so, b_so),
        (w_wkv, b_wkv),
        (w_wo, b_wo),
    )
    for i, (src, dst) in enumerate(order):
        copy = pltpu.make_async_copy(src, dst, load_sem.at[i])
        copy.start()
        loads.append(copy)
    l_lat, l_tok, l_rkv, l_rq, l_wq, l_ro, l_sqkv, l_so, l_wkv, l_wo = loads

    barrier = pltpu.get_barrier_semaphore()
    peers = [lax.rem(me + k, n) for k in range(1, n)]
    for peer in peers:
        pl.semaphore_signal(barrier, inc=1, device_id={"aa": peer}, device_id_type=MESH)

    row = lax.broadcasted_iota(jnp.int32, (TILE, TILE), 0) // width
    col = lax.broadcasted_iota(jnp.int32, (TILE, TILE), 1) // width
    mean_mat[...] = jnp.where(row == col, 1.0 / width, 0.0).astype(BF16)

    pl.semaphore_wait(barrier, n - 1)

    def remote(stage, k, src, dst):
        return pltpu.make_async_remote_copy(
            src_ref=src,
            dst_ref=dst,
            send_sem=send_sem.at[stage, k],
            recv_sem=recv_sem.at[stage, k],
            device_id={"aa": peers[k]},
            device_id_type=MESH,
        )

    gather_lat = [remote(0, k, latents, lat_all.at[mine]) for k in range(n - 1)]
    for copy in gather_lat:
        copy.start()

    def head_norm(y, index, tile, scale=None):
        mean = dot((y * y).astype(BF16), mean_mat[...])
        g = gain[index : index + 1, tile * TILE : (tile + 1) * TILE]
        if scale is not None:
            g = g * scale
        return (y * lax.rsqrt(mean + EPSILON) * g).astype(BF16)

    to_exp2 = math.log2(math.e) / math.sqrt(width)
    lane = lax.broadcasted_iota(jnp.int32, (1, LANES), 1)
    even = (lane < width).astype(F32)
    even_b, odd_b = even.astype(BF16), (1.0 - even).astype(BF16)

    def pair_attend(q, k, v):
        v1 = jnp.concatenate([v, jnp.ones_like(v)], axis=1)
        outs = []
        for mask in (even_b, odd_b):
            weights = jnp.exp2(dot_nt(q * mask, k)).astype(BF16)
            outs.append(dot(weights, v1))
        return outs

    def attend_into(q_ref, k_ref, v_ref, rows):
        pieces = []
        for p in range(pairs):
            cols = slice(p * LANES, (p + 1) * LANES)
            first, second = pair_attend(q_ref[rows, cols], k_ref[:, cols], v_ref[:, cols])
            num = jnp.where(lane < width, first[:, :LANES], second[:, :LANES])
            den = jnp.where(lane < width, first[:, LANES:], second[:, LANES:])
            pieces.append((num / den).astype(BF16))
        return jnp.concatenate(pieces, axis=1)

    l_tok.wait()
    ntok[...] = rms(tok[...])
    l_rkv.wait()
    for t in range(tiles):
        cols = slice(t * TILE, (t + 1) * TILE)
        rk[:, cols] = head_norm(dot(ntok[...], b_rkv[:, cols]), 1, t)
        vcols = slice(inner + t * TILE, inner + (t + 1) * TILE)
        rv[:, cols] = dot(ntok[...], b_rkv[:, vcols]).astype(BF16)

    l_lat.wait()
    l_rq.wait()
    for copy in gather_lat:
        copy.wait_recv()

    def read_queries(rows):
        normed[rows, :] = rms(lat_all[rows, :])
        for t in range(tiles):
            cols = slice(t * TILE, (t + 1) * TILE)
            rq[rows, cols] = head_norm(dot(normed[rows, :], b_rq[:, cols]), 0, t, to_exp2)

    row_blocks(every, read_queries)

    spread = LANES // HEADS

    def read_partial(rows):
        dens = None
        for p in range(pairs):
            cols = slice(p * LANES, (p + 1) * LANES)
            first, second = pair_attend(rq[rows, cols], rk[:, cols], rv[:, cols])
            part[rows, cols] = jnp.where(
                lane < width, first[:, :LANES], second[:, :LANES]
            ).astype(BF16)
            for j, one in enumerate((first, second)):
                head = 2 * p + j
                den = one[:, LANES:]
                dens = den if dens is None else jnp.where(lane >= head * spread, den, dens)
        part[rows, inner:] = dens.astype(BF16)

    row_blocks(every, read_partial)

    scatter = []
    for k in range(n - 1):
        theirs = pl.ds(pl.multiple_of(peers[k] * own, own), own)
        scatter.append(remote(1, k, part.at[theirs], recv.at[k]))
    for copy in scatter:
        copy.start()

    l_wq.wait()
    for t in range(tiles):
        cols = slice(t * TILE, (t + 1) * TILE)
        wq[:, cols] = head_norm(dot(ntok[...], b_wq[:, cols]), 4, t, to_exp2)

    pick_row = lax.broadcasted_iota(jnp.int32, (LANES, inner), 0)
    pick_col = lax.broadcasted_iota(jnp.int32, (LANES, inner), 1)
    pick = jnp.where(pick_row == (pick_col // width) * spread, 1.0, 0.0).astype(BF16)

    total = part[mine, :].astype(F32)
    for k in range(n - 1):
        scatter[k].wait_recv()
        total = total + recv[k].astype(F32)
    den = total[:, inner:]
    high = den.astype(BF16)
    low = (den - high.astype(F32)).astype(BF16)
    den = dot(high, pick) + dot(low, pick)
    att[mine, :] = (total[:, :inner] / den).astype(BF16)

    gather_att = [remote(2, k, att.at[mine], att.at[mine]) for k in range(n - 1)]
    for copy in gather_att:
        copy.start()

    l_ro.wait()
    l_sqkv.wait()
    for copy in gather_att:
        copy.wait_recv()

    def self_project(rows):
        new = lat_all[rows, :].astype(F32) + dot(att[rows, :], b_ro[...])
        new = new.astype(BF16)
        rlat[rows, :] = new
        normed[rows, :] = rms(new)
        for t in range(tiles):
            cols = slice(t * TILE, (t + 1) * TILE)
            for which, (ref, index, scale) in enumerate(
                ((sq, 2, to_exp2), (sk, 3, None), (sv, None, None))
            ):
                start = which * inner + t * TILE
                y = dot(normed[rows, :], b_sqkv[:, start : start + TILE])
                ref[rows, cols] = (
                    y.astype(BF16) if index is None else head_norm(y, index, t, scale)
                )

    row_blocks(every, self_project)

    l_so.wait()
    l_wkv.wait()

    def self_attend(rows):
        attended = attend_into(sq, sk, sv, rows)
        new = rlat[rows, :].astype(F32) + dot(attended, b_so[...])
        new = new.astype(BF16)
        rlat[rows, :] = new
        normed[rows, :] = rms(new)
        for t in range(tiles):
            cols = slice(t * TILE, (t + 1) * TILE)
            wk[rows, cols] = head_norm(dot(normed[rows, :], b_wkv[:, cols]), 5, t)
            vcols = slice(inner + t * TILE, inner + (t + 1) * TILE)
            wv[rows, cols] = dot(normed[rows, :], b_wkv[:, vcols]).astype(BF16)

    row_blocks(every, self_attend)
    lat_out[...] = rlat[mine, :]

    l_wo.wait()
    attended = attend_into(wq, wk, wv, slice(None))
    tok_out[...] = (tok[...].astype(F32) + dot(attended, b_wo[...])).astype(BF16)

    for copy in gather_lat + scatter + gather_att:
        copy.wait_send()


def per_device(n, tokens, latents, *weights_and_gain):
    weights, gain = weights_and_gain[:-1], weights_and_gain[-1]
    own, d = latents.shape
    count = tokens.shape[0]
    inner = weights[0].shape[1]
    every = n * own
    hbm = pl.BlockSpec(memory_space=pl.ANY)
    vmem = pl.BlockSpec(memory_space=pltpu.VMEM)

    def buf(*shape):
        return pltpu.VMEM(shape, BF16)

    return pl.pallas_call(
        functools.partial(kernel, n),
        out_shape=(
            jax.ShapeDtypeStruct(tokens.shape, BF16),
            jax.ShapeDtypeStruct(latents.shape, BF16),
        ),
        in_specs=[hbm] * 10 + [vmem],
        out_specs=(vmem, vmem),
        scratch_shapes=[
            buf(count, d),
            buf(every, d),
            *[buf(*w.shape) for w in weights],
            buf(count, d),
            buf(count, inner),
            buf(count, inner),
            buf(count, inner),
            buf(every, inner),
            buf(every, inner + LANES),
            buf(n - 1, own, inner + LANES),
            buf(every, inner),
            buf(every, d),
            buf(every, d),
            *[buf(every, inner) for _ in range(5)],
            buf(TILE, TILE),
            pltpu.SemaphoreType.DMA((10,)),
            pltpu.SemaphoreType.DMA((3, n - 1)),
            pltpu.SemaphoreType.DMA((3, n - 1)),
        ],
        compiler_params=pltpu.CompilerParams(
            collective_id=0, has_side_effects=True, vmem_limit_bytes=60 * 1024 * 1024
        ),
        name="rin_block",
    )(tokens, latents, *weights, gain)


def solution(mesh):
    rows = P(("ba", "aa"), None)
    return jax.shard_map(
        functools.partial(per_device, mesh.shape["aa"]),
        mesh=mesh,
        in_specs=(rows, rows) + (P(),) * 9,
        out_specs=(rows, rows),
        check_vma=False,
    )
```

time: 166 us -> 35 us (0.21)
  local copies, waits for them, and re-layouts: 51.8 us -> 3.24 us
  Pallas kernels: 0 us -> 30.9 us
  waiting for transfers between devices: 29.6 us -> 0 us
  blocking collectives: 25.2 us -> 0 us
  matrix products: 22.3 us -> 0 us
  other arithmetic: 21.3 us -> 0 us
  between operations: 14.3 us -> 0.64 us
    pallas_call x0 -> x1, Pallas kernels: none -> 30.9 us  [per_device(): pl.pallas_call(functools.partial(kernel, n), out_shape=(jax.ShapeDtypeStr...]
    psum x1 -> x0, waiting for transfers between devices: 29.6 us -> none  [per_device(): numerator, denominator = lax.psum((numerator, denominator), 'aa')]
    mul x18 -> x0, local copies, waits for them, and re-layouts: 27.6 us -> none  [the longest x12 16.5 us: head_norm(): split_heads * lax.rsqrt(jnp.mean(split_heads * split_heads, axis=-1, keep...]
    dot_general x14 -> x0, matrix products: 22.3 us -> none  [the longest x3 5.46 us: attend_block(): jnp.einsum('qhe,khe->hqk', query_heads, key_heads, preferred_element_type...]
    psum x1 -> x0, blocking collectives: 13.6 us -> none  [per_device(): numerator, denominator = lax.psum((numerator, denominator), 'aa')]
    all_gather x1 -> x0, blocking collectives: 11.6 us -> none  [per_device(): every_latent = lax.all_gather(latents, 'aa', axis=0, tiled=True)]
    convert_element_type x6 -> x0, other arithmetic: 11.3 us -> none  [the longest x5 10.2 us: head_norm(): return (normed.reshape(row_count, -1) * gain_row).astype(jnp.bfloat16)]
    convert_element_type x6 -> x0, local copies, waits for them, and re-layouts: 10.8 us -> none  [head_norm(): return (normed.reshape(row_count, -1) * gain_row).astype(jnp.bfloat16)]
  transfers between devices with their start and end apart: 1 -> 0, of which waited for: 1 -> 0; matrix products, arithmetic and copies ran while one was open for 7% -> 0% of each run, Pallas kernels for 0% -> 0%
where the time goes in v1:
time: 35 us; the launch traced here: 34.8 us
  Pallas kernels  30.9 us (88%)
  local copies, waits for them, and re-layouts  3.24 us (9%)
  between operations  0.64 us (2%)
    pallas_call x1, Pallas kernels, per_device(): pl.pallas_call(functools.partial(kernel, n), out_shape=(jax.ShapeDtypeStr...  30.9 us
    unnamed x2, local copies, waits for them, and re-layouts  3.24 us

profile of v1, /device:TPU:0, one launch (start us, length us, event | category | flops | bytes accessed | tf_op | source)
XLA Modules:
  0.0 34.8 jit_solution(15062965381108855766)
XLA Ops:
  0.6 30.9 %rin_block.1 = (bf16[192,1024]{1,0:T(8,128)(2,1)}, bf16[32,1024]{1,0:T(8,128)(2,1)}) custom-call(bf16[192,1024]{1,0:T(8,128)(2,1)} %tokens.1, bf16[32,1024]{1,0:T(8,128)(2,1)} %latents.1, bf16[1024,512]{1,0:T(8,128)(2,1)} %w_rq.1, bf16[1024,1024]{1,0:T(8,128)(2,1)} %w_rkv.1, bf16[512,1024]{1,0:T(8,128)(2,1)} %w_ro.1, bf16[1024,1536]{1,0:T(8,128)(2,1)} %w_sqkv.1, ...), custom_call_target="tpu_custom_call" | custom-call | tf_op jit(solution)/shard_map/rin_block/pallas_call | solution.py:306
  31.5 1.8 %copy.15 = bf16[192,1024]{1,0:T(8,128)(2,1)} copy(bf16[192,1024]{1,0:T(8,128)(2,1)} %get-tuple-element.4) | data formatting | bytes 786432
  33.3 1.5 %copy.16 = bf16[32,1024]{1,0:T(8,128)(2,1)} copy(bf16[32,1024]{1,0:T(8,128)(2,1)} %get-tuple-element.5) | data formatting | bytes 131072

commit v2 on v1

v2 whole, which is shorter than its diff:
```python
import functools
import math

import jax
import jax.numpy as jnp
from jax import lax
from jax.experimental import pallas as pl
from jax.experimental.pallas import tpu as pltpu
from jax.sharding import PartitionSpec as P

HEADS = 8
EPSILON = 1e-06
MESH = pl.DeviceIdType.MESH
TILE = 256
LANES = 128
F32 = jnp.float32
BF16 = jnp.bfloat16


def dot(a, b):
    return jnp.dot(a, b, preferred_element_type=F32)


def dot_nt(a, b):
    return lax.dot_general(a, b, (((1,), (1,)), ((), ())), preferred_element_type=F32)


def rms(x):
    x = x.astype(F32)
    return (x * lax.rsqrt(jnp.mean(x * x, axis=-1, keepdims=True) + EPSILON)).astype(BF16)


def row_blocks(rows, body):
    block = min(rows, TILE)
    if rows == block:
        body(pl.ds(0, block))
    else:

        def step(i, carry):
            body(pl.ds(pl.multiple_of(i * block, block), block))
            return carry

        lax.fori_loop(0, rows // block, step, 0)


def kernel(
    n,
    tokens,
    latents,
    w_rq,
    w_rkv,
    w_ro,
    w_sqkv,
    w_so,
    w_wq,
    w_wkv,
    w_wo,
    gain,
    tok_out,
    lat_out,
    tok,
    lat_all,
    b_rq,
    b_rkv,
    b_ro,
    b_sqkv,
    b_so,
    b_wq,
    b_wkv,
    b_wo,
    ntok,
    wq,
    q_send,
    q_all,
    kv_send,
    kv_all,
    heads_all,
    att,
    rlat,
    normed,
    sq,
    sk,
    sv,
    wk,
    wv,
    mean_mat,
    load_sem,
    send_sem,
    recv_sem,
):
    me = lax.axis_index("aa")
    own = latents.shape[0]
    every = n * own
    inner = w_rq.shape[1]
    width = inner // HEADS
    tiles = inner // TILE
    d = tokens.shape[1]
    pairs = inner // LANES

    count = tokens.shape[0]
    share = n // HEADS
    block = every // share
    half = block // 2
    chips = n // 2
    my_head = me // share

    barrier = pltpu.get_barrier_semaphore()
    peers = [lax.rem(me + k, n) for k in range(1, n)]
    sources = [lax.rem(me + n - k, n) for k in range(1, n)]
    partner = me + 1 - 2 * lax.rem(me, 2)
    for peer in peers:
        pl.semaphore_signal(barrier, inc=1, device_id={"aa": peer}, device_id_type=MESH)

    def rows_of(device, size):
        return pl.ds(pl.multiple_of(device * size, size), size)

    mine = rows_of(me, own)
    loads = []
    order = (
        (latents, lat_all.at[mine]),
        (w_rq, b_rq),
        (tokens, tok),
        (w_rkv, b_rkv),
        (w_wq, b_wq),
        (w_ro, b_ro),
        (w_sqkv, b_sqkv),
        (w_so, b_so),
        (w_wkv, b_wkv),
        (w_wo, b_wo),
    )
    for i, (src, dst) in enumerate(order):
        copy = pltpu.make_async_copy(src, dst, load_sem.at[i])
        copy.start()
        loads.append(copy)
    l_lat, l_rq, l_tok, l_rkv, l_wq, l_ro, l_sqkv, l_so, l_wkv, l_wo = loads

    row = lax.broadcasted_iota(jnp.int32, (TILE, TILE), 0) // width
    col = lax.broadcasted_iota(jnp.int32, (TILE, TILE), 1) // width
    mean_mat[...] = jnp.where(row == col, 1.0 / width, 0.0).astype(BF16)

    def remote(stage, k, src, dst, device):
        return pltpu.make_async_remote_copy(
            src_ref=src,
            dst_ref=dst,
            send_sem=send_sem.at[stage, k],
            recv_sem=recv_sem.at[stage, k],
            device_id={"aa": device},
            device_id_type=MESH,
        )

    def head_norm(y, index, tile, scale=None):
        mean = dot((y * y).astype(BF16), mean_mat[...])
        g = gain[index : index + 1, tile * TILE : (tile + 1) * TILE]
        if scale is not None:
            g = g * scale
        return y * lax.rsqrt(mean + EPSILON) * g

    to_exp2 = math.log2(math.e) / math.sqrt(width)
    lane = lax.broadcasted_iota(jnp.int32, (1, LANES), 1)
    low = lane < width
    even_b = low.astype(F32).astype(BF16)
    odd_b = (1.0 - low.astype(F32)).astype(BF16)
    per_tile = TILE // LANES

    def pair_attend(q, k, v):
        v1 = jnp.concatenate([v, jnp.ones_like(v)], axis=1)
        outs = []
        for mask in (even_b, odd_b):
            weights = jnp.exp2(dot_nt(q * mask, k)).astype(BF16)
            outs.append(dot(weights, v1))
        return outs

    def attend_into(q_ref, k_ref, v_ref, rows):
        pieces = []
        for p in range(pairs):
            cols = slice(p * LANES, (p + 1) * LANES)
            first, second = pair_attend(q_ref[rows, cols], k_ref[:, cols], v_ref[:, cols])
            num = jnp.where(low, first[:, :LANES], second[:, :LANES])
            den = jnp.where(low, first[:, LANES:], second[:, LANES:])
            pieces.append((num / den).astype(BF16))
        return jnp.concatenate(pieces, axis=1)

    l_lat.wait()
    l_rq.wait()
    own_normed = rms(lat_all[mine, :])
    for t in range(tiles):
        cols = slice(t * TILE, (t + 1) * TILE)
        q = head_norm(dot(own_normed, b_rq[:, cols]), 0, t, to_exp2).astype(BF16)
        for j in range(per_tile):
            q_send[t * per_tile + j] = q[:, j * LANES : (j + 1) * LANES]
    q_all[mine, :] = q_send[my_head // 2]

    pl.semaphore_wait(barrier, n - 1)

    send_q = [
        remote(0, k, q_send.at[peers[k] // (2 * share)], q_all.at[mine], peers[k])
        for k in range(n - 1)
    ]
    for copy in send_q:
        copy.start()

    l_tok.wait()
    ntok[...] = rms(tok[...])
    l_rkv.wait()
    for t in range(tiles):
        cols = slice(t * TILE, (t + 1) * TILE)
        vcols = slice(inner + t * TILE, inner + (t + 1) * TILE)
        keys = head_norm(dot(ntok[...], b_rkv[:, cols]), 1, t)
        values = dot(ntok[...], b_rkv[:, vcols])
        for j in range(per_tile):
            part = slice(j * LANES, (j + 1) * LANES)
            k, v = keys[:, part], pltpu.roll(values[:, part], width, 1)
            head = 2 * (t * per_tile + j)
            kv_send[head] = jnp.where(low, k, v).astype(BF16)
            kv_send[head + 1] = jnp.where(low, v, k).astype(BF16)
    my_tokens = rows_of(me, count)
    send_kv = [
        remote(1, k, kv_send.at[peers[k] // share], kv_all.at[my_tokens], peers[k])
        for k in range(n - 1)
    ]
    for copy in send_kv:
        copy.start()
    kv_all[my_tokens, :] = kv_send[my_head]

    send_lat = [
        remote(2, j - 1, latents, lat_all.at[mine], lax.rem(me + 2 * j, n))
        for j in range(1, chips)
    ]
    send_lat.append(remote(2, chips - 1, latents, lat_all.at[mine], partner))
    for copy in send_lat:
        copy.start()

    l_wq.wait()
    for t in range(tiles):
        cols = slice(t * TILE, (t + 1) * TILE)
        wq[:, cols] = head_norm(dot(ntok[...], b_wq[:, cols]), 4, t, to_exp2).astype(BF16)

    for copy in send_q:
        copy.wait_recv()
    parity = lax.rem(my_head, 2)
    mine_b = jnp.where(lane // width == parity, 1.0, 0.0).astype(BF16)
    q = q_all[rows_of(lax.rem(me, share), block), :] * mine_b
    total = None
    for k in range(n):
        if k:
            send_kv[k - 1].wait_recv()
        kv = kv_all[rows_of(sources[k - 1] if k else me, count), :]
        weights = jnp.exp2(dot_nt(q, kv)).astype(BF16)
        term = dot(weights, jnp.concatenate([kv, jnp.ones_like(kv)], axis=1))
        total = term if total is None else total + term
    quotient = total[:, :LANES] / total[:, LANES:]
    message = jnp.where(
        lane // width == parity, pltpu.roll(quotient[:half], width, 1), quotient[half:]
    )
    heads_all[me] = message.astype(BF16)
    gather_att = [
        remote(3, k, heads_all.at[me], heads_all.at[me], peers[k]) for k in range(n - 1)
    ]
    for copy in gather_att:
        copy.start()

    relay_lat = []
    for j in range(1, chips):
        send_lat[j - 1].wait_recv()
        theirs = rows_of(lax.rem(me + n - 2 * j, n), own)
        copy = remote(2, chips - 1 + j, lat_all.at[theirs], lat_all.at[theirs], partner)
        copy.start()
        relay_lat.append(copy)
    send_lat[chips - 1].wait_recv()
    for copy in relay_lat:
        copy.wait_recv()

    l_ro.wait()
    l_sqkv.wait()
    for copy in gather_att:
        copy.wait_recv()
    for p in range(pairs):
        cols = slice(p * LANES, (p + 1) * LANES)
        for b in range(share):
            first = heads_all[2 * p * share + b].astype(F32)
            second = heads_all[(2 * p + 1) * share + b].astype(F32)
            top = jnp.where(low, first, second)
            bottom = pltpu.roll(jnp.where(low, second, first), width, 1)
            att[b * block : b * block + half, cols] = top.astype(BF16)
            att[b * block + half : (b + 1) * block, cols] = bottom.astype(BF16)

    def self_project(rows):
        new = lat_all[rows, :].astype(F32) + dot(att[rows, :], b_ro[...])
        new = new.astype(BF16)
        rlat[rows, :] = new
        normed[rows, :] = rms(new)
        for t in range(tiles):
            cols = slice(t * TILE, (t + 1) * TILE)
            for which, (ref, index, scale) in enumerate(
                ((sq, 2, to_exp2), (sk, 3, None), (sv, None, None))
            ):
                start = which * inner + t * TILE
                y = dot(normed[rows, :], b_sqkv[:, start : start + TILE])
                y = y if index is None else head_norm(y, index, t, scale)
                ref[rows, cols] = y.astype(BF16)

    row_blocks(every, self_project)

    l_so.wait()
    l_wkv.wait()

    def self_attend(rows):
        attended = attend_into(sq, sk, sv, rows)
        new = rlat[rows, :].astype(F32) + dot(attended, b_so[...])
        new = new.astype(BF16)
        rlat[rows, :] = new
        normed[rows, :] = rms(new)
        for t in range(tiles):
            cols = slice(t * TILE, (t + 1) * TILE)
            wk[rows, cols] = head_norm(dot(normed[rows, :], b_wkv[:, cols]), 5, t).astype(BF16)
            vcols = slice(inner + t * TILE, inner + (t + 1) * TILE)
            wv[rows, cols] = dot(normed[rows, :], b_wkv[:, vcols]).astype(BF16)

    row_blocks(every, self_attend)
    lat_out[...] = rlat[mine, :]

    l_wo.wait()
    attended = attend_into(wq, wk, wv, slice(None))
    tok_out[...] = (tok[...].astype(F32) + dot(attended, b_wo[...])).astype(BF16)

    for copy in send_q + send_kv + send_lat + relay_lat + gather_att:
        copy.wait_send()


def per_device(n, tokens, latents, *weights_and_gain):
    weights, gain = weights_and_gain[:-1], weights_and_gain[-1]
    own, d = latents.shape
    count = tokens.shape[0]
    inner = weights[0].shape[1]
    every = n * own
    hbm = pl.BlockSpec(memory_space=pl.ANY)
    vmem = pl.BlockSpec(memory_space=pltpu.VMEM)

    def buf(*shape):
        return pltpu.VMEM(shape, BF16)

    return pl.pallas_call(
        functools.partial(kernel, n),
        out_shape=(
            pltpu.VMEM(tokens.shape, BF16),
            pltpu.VMEM(latents.shape, BF16),
        ),
        in_specs=[hbm] * 10 + [vmem],
        out_specs=(vmem, vmem),
        scratch_shapes=[
            buf(count, d),
            buf(every, d),
            *[buf(*w.shape) for w in weights],
            buf(count, d),
            buf(count, inner),
            buf(inner // LANES, own, LANES),
            buf(every, LANES),
            buf(HEADS, count, LANES),
            buf(n * count, LANES),
            buf(n, every * HEADS // n // 2, LANES),
            buf(every, inner),
            buf(every, d),
            buf(every, d),
            *[buf(every, inner) for _ in range(5)],
            buf(TILE, TILE),
            pltpu.SemaphoreType.DMA((10,)),
            pltpu.SemaphoreType.DMA((4, n - 1)),
            pltpu.SemaphoreType.DMA((4, n - 1)),
        ],
        compiler_params=pltpu.CompilerParams(
            collective_id=0, has_side_effects=True, vmem_limit_bytes=67043328 - 1000 * 1024
        ),
        name="rin_block",
    )(tokens, latents, *weights, gain)


def solution(mesh):
    rows = P(("ba", "aa"), None)
    return jax.shard_map(
        functools.partial(per_device, mesh.shape["aa"]),
        mesh=mesh,
        in_specs=(rows, rows) + (P(),) * 9,
        out_specs=(rows, rows),
        check_vma=False,
    )
```

time: 35 us -> 26.5 us (0.76)
  Pallas kernels: 30.9 us -> 24.3 us
  local copies, waits for them, and re-layouts: 3.24 us -> 1.38 us
    pallas_call x1, Pallas kernels: 30.9 us -> 24.3 us  [per_device(): pl.pallas_call(functools.partial(kernel, n), out_shape=(pltpu.VMEM(tokens...]
    unnamed x2, local copies, waits for them, and re-layouts: 3.24 us -> 1.38 us
where the time goes in v2:
time: 26.5 us; the launch traced here: 26.3 us
  Pallas kernels  24.3 us (92%)
  local copies, waits for them, and re-layouts  1.38 us (5%)
  between operations  0.64 us (2%)
    pallas_call x1, Pallas kernels, per_device(): pl.pallas_call(functools.partial(kernel, n), out_shape=(pltpu.VMEM(tokens...  24.3 us
    unnamed x2, local copies, waits for them, and re-layouts  1.38 us

profile of v2, /device:TPU:0, one launch (start us, length us, event | category | flops | bytes accessed | tf_op | source)
XLA Modules:
  0.0 26.3 jit_solution(18121685698568266413)
XLA Ops:
  0.6 24.3 %rin_block.1 = (bf16[192,1024]{1,0:T(8,128)(2,1)S(1)}, bf16[32,1024]{1,0:T(8,128)(2,1)S(1)}) custom-call(bf16[192,1024]{1,0:T(8,128)(2,1)} %tokens.1, bf16[32,1024]{1,0:T(8,128)(2,1)} %latents.1, bf16[1024,512]{1,0:T(8,128)(2,1)} %w_rq.1, bf16[1024,1024]{1,0:T(8,128)(2,1)} %w_rkv.1, bf16[512,1024]{1,0:T(8,128)(2,1)} %w_ro.1, bf16[1024,1536]{1,0:T(8,128)(2,1)} %w_sqkv.1, ...), custom_call_target="tpu_custom_call" | custom-call | tf_op jit(solution)/shard_map/rin_block/pallas_call | solution.py:342
  24.9 0.7 %copy.15 = bf16[192,1024]{1,0:T(8,128)(2,1)} copy(bf16[192,1024]{1,0:T(8,128)(2,1)S(1)} %get-tuple-element.2) | data formatting | bytes 786432
  25.7 0.6 %copy.16 = bf16[32,1024]{1,0:T(8,128)(2,1)} copy(bf16[32,1024]{1,0:T(8,128)(2,1)S(1)} %get-tuple-element.3) | data formatting | bytes 131072

commit v3 on v2

--- a/solution.py
+++ b/solution.py
@@ -190,15 +190,6 @@
             q_send[t * per_tile + j] = q[:, j * LANES : (j + 1) * LANES]
     q_all[mine, :] = q_send[my_head // 2]
 
-    pl.semaphore_wait(barrier, n - 1)
-
-    send_q = [
-        remote(0, k, q_send.at[peers[k] // (2 * share)], q_all.at[mine], peers[k])
-        for k in range(n - 1)
-    ]
-    for copy in send_q:
-        copy.start()
-
     l_tok.wait()
     ntok[...] = rms(tok[...])
     l_rkv.wait()
@@ -213,6 +204,15 @@
             head = 2 * (t * per_tile + j)
             kv_send[head] = jnp.where(low, k, v).astype(BF16)
             kv_send[head + 1] = jnp.where(low, v, k).astype(BF16)
+    pl.semaphore_wait(barrier, n - 1)
+
+    send_q = [
+        remote(0, k, q_send.at[peers[k] // (2 * share)], q_all.at[mine], peers[k])
+        for k in range(n - 1)
+    ]
+    for copy in send_q:
+        copy.start()
+
     my_tokens = rows_of(me, count)
     send_kv = [
         remote(1, k, kv_send.at[peers[k] // share], kv_all.at[my_tokens], peers[k])

time: 26.5 us -> 27.2 us (1.026)
  Pallas kernels: 24.3 us -> 25 us
    pallas_call x1, Pallas kernels: 24.3 us -> 25 us  [per_device(): pl.pallas_call(functools.partial(kernel, n), out_shape=(pltpu.VMEM(tokens...]
where the time goes in v3:
time: 27.2 us; the launch traced here: 27 us
  Pallas kernels  25 us (92%)
  local copies, waits for them, and re-layouts  1.38 us (5%)
  between operations  0.64 us (2%)
    pallas_call x1, Pallas kernels, per_device(): pl.pallas_call(functools.partial(kernel, n), out_shape=(pltpu.VMEM(tokens...  25 us
    unnamed x2, local copies, waits for them, and re-layouts  1.38 us

profile of v3, /device:TPU:0, one launch (start us, length us, event | category | flops | bytes accessed | tf_op | source)
XLA Modules:
  0.0 27.0 jit_solution(13359197919848079256)
XLA Ops:
  0.6 25.0 %rin_block.1 = (bf16[192,1024]{1,0:T(8,128)(2,1)S(1)}, bf16[32,1024]{1,0:T(8,128)(2,1)S(1)}) custom-call(bf16[192,1024]{1,0:T(8,128)(2,1)} %tokens.1, bf16[32,1024]{1,0:T(8,128)(2,1)} %latents.1, bf16[1024,512]{1,0:T(8,128)(2,1)} %w_rq.1, bf16[1024,1024]{1,0:T(8,128)(2,1)} %w_rkv.1, bf16[512,1024]{1,0:T(8,128)(2,1)} %w_ro.1, bf16[1024,1536]{1,0:T(8,128)(2,1)} %w_sqkv.1, ...), custom_call_target="tpu_custom_call" | custom-call | tf_op jit(solution)/shard_map/rin_block/pallas_call | solution.py:342
  25.6 0.7 %copy.15 = bf16[192,1024]{1,0:T(8,128)(2,1)} copy(bf16[192,1024]{1,0:T(8,128)(2,1)S(1)} %get-tuple-element.2) | data formatting | bytes 786432
  26.4 0.6 %copy.16 = bf16[32,1024]{1,0:T(8,128)(2,1)} copy(bf16[32,1024]{1,0:T(8,128)(2,1)S(1)} %get-tuple-element.3) | data formatting | bytes 131072

commit v4 on v2

--- a/solution.py
+++ b/solution.py
@@ -199,6 +199,11 @@
     for copy in send_q:
         copy.start()
 
+    my_tokens = rows_of(me, count)
+    send_kv = [
+        remote(1, k, kv_send.at[peers[k] // share], kv_all.at[my_tokens], peers[k])
+        for k in range(n - 1)
+    ]
     l_tok.wait()
     ntok[...] = rms(tok[...])
     l_rkv.wait()
@@ -213,13 +218,8 @@
             head = 2 * (t * per_tile + j)
             kv_send[head] = jnp.where(low, k, v).astype(BF16)
             kv_send[head + 1] = jnp.where(low, v, k).astype(BF16)
-    my_tokens = rows_of(me, count)
-    send_kv = [
-        remote(1, k, kv_send.at[peers[k] // share], kv_all.at[my_tokens], peers[k])
-        for k in range(n - 1)
-    ]
-    for copy in send_kv:
-        copy.start()
+        for k in range(n - 1):
+            pl.when(peers[k] // (share * 2 * per_tile) == t)(send_kv[k].start)
     kv_all[my_tokens, :] = kv_send[my_head]
 
     send_lat = [

time: 26.5 us -> 27.1 us (1.023)
  Pallas kernels: 24.3 us -> 24.8 us
    pallas_call x1, Pallas kernels: 24.3 us -> 24.8 us  [per_device(): pl.pallas_call(functools.partial(kernel, n), out_shape=(pltpu.VMEM(tokens...]
where the time goes in v4:
time: 27.1 us; the launch traced here: 26.8 us
  Pallas kernels  24.8 us (92%)
  local copies, waits for them, and re-layouts  1.38 us (5%)
  between operations  0.64 us (2%)
    pallas_call x1, Pallas kernels, per_device(): pl.pallas_call(functools.partial(kernel, n), out_shape=(pltpu.VMEM(tokens...  24.8 us
    unnamed x2, local copies, waits for them, and re-layouts  1.38 us

profile of v4, /device:TPU:0, one launch (start us, length us, event | category | flops | bytes accessed | tf_op | source)
XLA Modules:
  0.0 26.8 jit_solution(9509876702508200001)
XLA Ops:
  0.6 24.8 %rin_block.1 = (bf16[192,1024]{1,0:T(8,128)(2,1)S(1)}, bf16[32,1024]{1,0:T(8,128)(2,1)S(1)}) custom-call(bf16[192,1024]{1,0:T(8,128)(2,1)} %tokens.1, bf16[32,1024]{1,0:T(8,128)(2,1)} %latents.1, bf16[1024,512]{1,0:T(8,128)(2,1)} %w_rq.1, bf16[1024,1024]{1,0:T(8,128)(2,1)} %w_rkv.1, bf16[512,1024]{1,0:T(8,128)(2,1)} %w_ro.1, bf16[1024,1536]{1,0:T(8,128)(2,1)} %w_sqkv.1, ...), custom_call_target="tpu_custom_call" | custom-call | tf_op jit(solution)/shard_map/rin_block/pallas_call | solution.py:342
  25.4 0.7 %copy.15 = bf16[192,1024]{1,0:T(8,128)(2,1)} copy(bf16[192,1024]{1,0:T(8,128)(2,1)S(1)} %get-tuple-element.2) | data formatting | bytes 786432
  26.2 0.6 %copy.16 = bf16[32,1024]{1,0:T(8,128)(2,1)} copy(bf16[32,1024]{1,0:T(8,128)(2,1)S(1)} %get-tuple-element.3) | data formatting | bytes 131072
